TPU v7x, 512 devices: a whole 4x4x16 slice. The times are simulated.
512 devices in a mesh: gz: 16 (over z), gy: 32 (over x, y, core).
Axes of the slice: x: 4, y: 4, z: 16, core: 2. Of those that a mesh axis runs over, the one named last changes fastest.
Arguments:
- tracer: float32 [512, 1024, 128], P('gz', 'gy'), may hold values from 0.1 to 10
- y_speed: float32 [512, 1024, 128], P('gz', 'gy'), may hold values from -0.4 to 0.4
- z_speed: float32 [512, 1024, 128], P('gz', 'gy'), may hold values from -0.4 to 0.4
- kappa: float32 [512, 1024, 128], P('gz', 'gy'), may hold values from 0.5 to 8
Outputs:
- updated: float32 [512, 1024, 128], P('gz', 'gy')
All inputs are finite; a program needn't handle non-finite values.
Results may differ from a plain program's by a relative error of at most 0.0003.
Values sent between devices are 32-bit elements; how exact they have to be, the bound alone decides.
A program may use at most 64 MiB of HBM per device.

v0:
```python
import jax
import jax.numpy as jnp
from jax import lax
from jax.sharding import PartitionSpec as P

NSUB = 4


rate_const = 500.0


def padded_2(x, sides, width):
    for axis, dim in sides:
        peers, length = (lax.axis_size(axis), x.shape[dim])
        up = [(i, (i + 1) % peers) for i in range(peers - 1)]
        down = [(j, i) for i, j in up]
        last = lax.slice_in_dim(x, length - width, length, axis=dim)
        leading = lax.slice_in_dim(x, 0, width, axis=dim)
        before = lax.ppermute(last, axis, up)
        after = lax.ppermute(leading, axis, down)
        x = jnp.concatenate([before, x, after], axis=dim)
    return x


def from_behind(x, axis, by):
    peers = lax.axis_size(axis)
    pairs = [(i, i + by) for i in range(peers) if 0 <= i + by < peers]
    return lax.ppermute(x, axis, pairs)


def advect_once(tracer, y_speed, z_speed):
    face_y = 0.5 * (y_speed[:, 1:] + y_speed[:, :-1])
    flux_y = jnp.maximum(face_y, 0.0) * tracer[:, :-1] + jnp.minimum(face_y, 0.0) * tracer[:, 1:]
    diff_y = flux_y[:, 1:] - flux_y[:, :-1]
    face_z = 0.5 * (z_speed[1:] + z_speed[:-1])
    flux_z = jnp.maximum(face_z, 0.0) * tracer[:-1] + jnp.minimum(face_z, 0.0) * tracer[1:]
    diff_z = flux_z[1:] - flux_z[:-1]
    return tracer[1:-1, 1:-1] - diff_y[1:-1] - diff_z[:, 1:-1]


def move_down(values, offset, axis, fill):
    count = values.shape[axis]
    kept = lax.slice_in_dim(values, 0, count - offset, axis=axis)
    padding = jnp.full_like(lax.slice_in_dim(values, 0, offset, axis=axis), fill)
    return jnp.concatenate([padding, kept], axis=axis)


def move_up(values, offset, axis, fill):
    count = values.shape[axis]
    kept = lax.slice_in_dim(values, offset, count, axis=axis)
    padding = jnp.full_like(lax.slice_in_dim(values, 0, offset, axis=axis), fill)
    return jnp.concatenate([kept, padding], axis=axis)


def reduce_lines(sub_diag, main_diag, sup_diag, rights, axis):
    count = main_diag.shape[axis]
    offset = 1
    while offset < count:
        factor_low = -sub_diag / move_down(main_diag, offset, axis, 1.0)
        factor_high = -sup_diag / move_up(main_diag, offset, axis, 1.0)
        new_main = (
            main_diag
            + factor_low * move_down(sup_diag, offset, axis, 0.0)
            + factor_high * move_up(sub_diag, offset, axis, 0.0)
        )
        new_sub = factor_low * move_down(sub_diag, offset, axis, 0.0)
        new_sup = factor_high * move_up(sup_diag, offset, axis, 0.0)
        rights = tuple(
            (
                right
                + factor_low * move_down(right, offset, axis, 0.0)
                + factor_high * move_up(right, offset, axis, 0.0)
                for right in rights
            )
        )
        sub_diag, main_diag, sup_diag = (new_sub, new_main, new_sup)
        offset = offset * 2
    return tuple((right / main_diag for right in rights))


def solve_rows(items):
    tracer_part, kappa_part = items
    count = kappa_part.shape[1]
    inner = rate_const * 0.5 * (kappa_part[:, 1:] + kappa_part[:, :-1])
    lower = jnp.concatenate([rate_const * kappa_part[:, :1], inner], axis=1)
    upper = jnp.concatenate([inner, rate_const * kappa_part[:, count - 1 :]], axis=1)
    main_diag = 1.0 + lower + upper
    zero_row = jnp.zeros_like(kappa_part[:, :1])
    sub_diag = jnp.concatenate([zero_row, -inner], axis=1)
    sup_diag = jnp.concatenate([-inner, zero_row], axis=1)
    solved = reduce_lines(sub_diag, main_diag, sup_diag, (tracer_part,), 1)[0]
    return lax.all_to_all(solved, "gy", split_axis=1, concat_axis=0, tiled=True)


def local(tracer, y_speed, z_speed, kappa):
    depth_z, depth_y, band = tracer.shape
    z_index = lax.axis_index("gz")
    z_count = lax.axis_size("gz")
    fields = jnp.stack([y_speed, z_speed, kappa])
    width = 1
    padded = padded_2(fields, (("gz", 1), ("gy", 2)), 1)
    state = tracer
    for step in range(NSUB):
        rimmed = padded_2(state, (("gz", 0), ("gy", 1)), 1)
        state = advect_once(rimmed, padded[0], padded[1])
    kappa_below = padded[2, width - 1 : width, width : width + depth_y]
    kappa_above = padded[2, width + depth_z : width + depth_z + 1, width : width + depth_y]
    lines = solve_rows(
        (
            lax.all_to_all(state, "gy", split_axis=0, concat_axis=1, tiled=True),
            lax.all_to_all(kappa, "gy", split_axis=0, concat_axis=1, tiled=True),
        )
    )
    inner = rate_const * 0.5 * (kappa[1:] + kappa[:-1])
    low_edge = jnp.where(
        z_index == 0, rate_const * kappa[:1], rate_const * 0.5 * (kappa[:1] + kappa_below)
    )
    high_edge = jnp.where(
        z_index == z_count - 1,
        rate_const * kappa[depth_z - 1 :],
        rate_const * 0.5 * (kappa[depth_z - 1 :] + kappa_above),
    )
    lower = jnp.concatenate([low_edge, inner], axis=0)
    upper = jnp.concatenate([inner, high_edge], axis=0)
    main_diag = 1.0 + lower + upper
    inner_count = depth_z - 1
    zero_row = jnp.zeros_like(kappa[:1])
    sub_local = jnp.concatenate([zero_row, -lower[1:inner_count]], axis=0)
    sup_local = jnp.concatenate([-upper[: inner_count - 1], zero_row], axis=0)
    zero_rows = jnp.zeros_like(kappa[: inner_count - 1])
    first_right = jnp.concatenate([lower[:1], zero_rows], axis=0)
    last_right = jnp.concatenate([zero_rows, upper[inner_count - 1 : inner_count]], axis=0)
    base, toward_low, toward_high = reduce_lines(
        sub_local,
        main_diag[:inner_count],
        sup_local,
        (lines[:inner_count], first_right, last_right),
        0,
    )
    following = from_behind(jnp.stack([base[0], toward_low[0], toward_high[0]]), "gz", -1)
    sep_low = lower[depth_z - 1]
    sep_high = upper[depth_z - 1]
    sub_red = jnp.where(z_index == 0, 0.0, -sep_low * toward_low[inner_count - 1])
    diag_red = (
        main_diag[depth_z - 1] - sep_low * toward_high[inner_count - 1] - sep_high * following[1]
    )
    sup_red = -sep_high * following[2]
    rhs_red = lines[depth_z - 1] + sep_low * base[inner_count - 1] + sep_high * following[0]
    equations = jnp.stack([sub_red, diag_red, sup_red, rhs_red])
    collected = lax.all_gather(equations[None], "gz", axis=0, tiled=True)
    values = reduce_lines(collected[:, 0], collected[:, 1], collected[:, 2], (collected[:, 3],), 0)[
        0
    ]
    sep_here = lax.dynamic_index_in_dim(values, z_index, axis=0, keepdims=False)
    previous = lax.dynamic_index_in_dim(values, jnp.maximum(z_index - 1, 0), axis=0, keepdims=False)
    sep_prev = jnp.where(z_index > 0, previous, 0.0)
    interior = base + sep_prev[None] * toward_low + sep_here[None] * toward_high
    return jnp.concatenate([interior, sep_here[None]], axis=0)


def solution(mesh):
    return jax.shard_map(
        local,
        mesh=mesh,
        in_specs=(
            P("gz", "gy", None),
            P("gz", "gy", None),
            P("gz", "gy", None),
            P("gz", "gy", None),
        ),
        out_specs=P("gz", "gy", None),
        check_vma=False,
    )
```

profile of v0, /device:TPU:24, one launch (start us, length us, event | category | flops | bytes accessed | tf_op | source)
XLA Modules:
  0.0 254.6 jit_solution(3350201011597019658)
XLA Ops:
  7.4 3.8 %collective-permute-start.4 = (f32[1,32,128]{2,1,0:T(8,128)S(1)}, f32[1,32,128]{2,1,0:T(8,128)S(1)}, u32[]{:S(2)}, u32[]{:S(2)}) collective-permute-start(f32[1,32,128]{2,1,0:T(8,128)S(1)} %get-tuple-element.204), channel_id=1, source_target_pairs={{0,32},{32,64},{64,96},{96,128},{128,160},{160,192},{192,224},{224... | collective-permute-start | bytes 49160 | tf_op jit(solution)/shard_map/ppermute | solution.py:19
  12.0 3.8 %collective-permute-start = (f32[3,1,32,128]{3,2,1,0:T(8,128)S(1)}, f32[3,1,32,128]{3,2,1,0:T(8,128)S(1)}, u32[]{:S(2)}, u32[]{:S(2)}) collective-permute-start(f32[3,1,32,128]{3,2,1,0:T(8,128)S(1)} %get-tuple-element.65), channel_id=1, source_target_pairs={{0,32},{32,64},{64,96},{96,128},{128,160},{160,192},{192,224},{224... | collective-permute-start | bytes 147464 | tf_op jit(solution)/shard_map/ppermute | solution.py:19
  15.9 1.3 collective-permute-start.1
  17.2 1.3 collective-permute-start.5
  18.5 4.9 %collective-permute-done.5 = f32[1,32,128]{2,1,0:T(8,128)S(1)} collective-permute-done((f32[1,32,128]{2,1,0:T(8,128)S(1)}, f32[1,32,128]{2,1,0:T(8,128)S(1)}, u32[]{:S(2)}, u32[]{:S(2)}) %collective-permute-start.5) | collective-permute-done | bytes 16416 | tf_op jit(solution)/shard_map/ppermute | solution.py:20
  23.5 1.9 collective-permute-start.6
  25.4 3.6 %collective-permute-start.7 = (f32[34,1,128]{2,1,0:T(1,128)S(1)}, f32[34,1,128]{2,1,0:T(1,128)S(1)}, u32[]{:S(2)}, u32[]{:S(2)}) collective-permute-start(f32[34,1,128]{2,1,0:T(1,128)S(1)} %get-tuple-element.114), channel_id=1, source_target_pairs={{1,0},{2,1},{3,2},{4,3},{5,4},{6,5},{7,6},{8,7},{9,8},{10,9},{11,1... | collective-permute-start | bytes 52232 | tf_op jit(solution)/shard_map/ppermute | solution.py:20
  30.1 1.9 collective-permute-start.2
  32.1 3.6 %collective-permute-start.3 = (f32[3,34,1,128]{3,2,1,0:T(1,128)S(1)}, f32[3,34,1,128]{3,2,1,0:T(1,128)S(1)}, u32[]{:S(2)}, u32[]{:S(2)}) collective-permute-start(f32[3,34,1,128]{3,2,1,0:T(1,128)S(1)} %get-tuple-element.62), channel_id=1, source_target_pairs={{1,0},{2,1},{3,2},{4,3},{5,4},{6,5},{7,6},{8,7},{9,8},{10,9},{11,1... | collective-permute-start | bytes 156680 | tf_op jit(solution)/shard_map/ppermute | solution.py:20
  35.8 2.2 collective-permute-done.3
  38.1 1.4 pad_maximum_fusion
  40.5 4.9 %collective-permute-start.8 = (f32[1,32,128]{2,1,0:T(8,128)S(1)}, f32[1,32,128]{2,1,0:T(8,128)S(1)}, u32[]{:S(2)}, u32[]{:S(2)}) collective-permute-start(f32[1,32,128]{2,1,0:T(8,128)S(1)} %get-tuple-element.201), channel_id=1, source_target_pairs={{0,32},{32,64},{64,96},{96,128},{128,160},{160,192},{192,224},{224... | collective-permute-start | bytes 49160 | tf_op jit(solution)/shard_map/ppermute | solution.py:19
  45.5 1.3 collective-permute-start.9
  46.8 11.1 %all-to-all-start.1 = ((f32[32,32,128]{2,1,0:T(8,128)}), f32[32,32,128]{2,1,0:T(8,128)S(1)}, u32[]{:S(2)}, u32[]{:S(2)}) async-start(f32[32,32,128]{2,1,0:T(8,128)} %param.7), calls=%async_computation.1 | async-start | bytes 1048576 | tf_op jit(solution)/shard_map/all_to_all | solution.py:111
  57.9 2.0 collective-permute-start.10
  59.9 3.5 %collective-permute-start.11 = (f32[34,1,128]{2,1,0:T(1,128)S(1)}, f32[34,1,128]{2,1,0:T(1,128)S(1)}, u32[]{:S(2)}, u32[]{:S(2)}) collective-permute-start(f32[34,1,128]{2,1,0:T(1,128)S(1)} %get-tuple-element.112), channel_id=1, source_target_pairs={{1,0},{2,1},{3,2},{4,3},{5,4},{6,5},{7,6},{8,7},{9,8},{10,9},{11,1... | collective-permute-start | bytes 52232 | tf_op jit(solution)/shard_map/ppermute | solution.py:20
  65.8 4.6 %collective-permute-start.12 = (f32[1,32,128]{2,1,0:T(8,128)S(1)}, f32[1,32,128]{2,1,0:T(8,128)S(1)}, u32[]{:S(2)}, u32[]{:S(2)}) collective-permute-start(f32[1,32,128]{2,1,0:T(8,128)S(1)} %get-tuple-element.199), channel_id=1, source_target_pairs={{0,32},{32,64},{64,96},{96,128},{128,160},{160,192},{192,224},{224... | collective-permute-start | bytes 49160 | tf_op jit(solution)/shard_map/ppermute | solution.py:19
  70.4 1.3 collective-permute-start.13
  71.8 5.4 %collective-permute-done.13 = f32[1,32,128]{2,1,0:T(8,128)S(1)} collective-permute-done((f32[1,32,128]{2,1,0:T(8,128)S(1)}, f32[1,32,128]{2,1,0:T(8,128)S(1)}, u32[]{:S(2)}, u32[]{:S(2)}) %collective-permute-start.13) | collective-permute-done | bytes 16416 | tf_op jit(solution)/shard_map/ppermute | solution.py:20
  77.3 4.4 %collective-permute-start.14 = (f32[34,1,128]{2,1,0:T(1,128)S(1)}, f32[34,1,128]{2,1,0:T(1,128)S(1)}, u32[]{:S(2)}, u32[]{:S(2)}) collective-permute-start(f32[34,1,128]{2,1,0:T(1,128)S(1)} %get-tuple-element.109), channel_id=1, source_target_pairs={{0,1},{1,2},{2,3},{3,4},{4,5},{5,6},{6,7},{7,8},{8,9},{9,10},{10,1... | collective-permute-start | bytes 52232 | tf_op jit(solution)/shard_map/ppermute | solution.py:19
  81.7 1.9 collective-permute-start.15
  86.7 3.9 %collective-permute-start.16 = (f32[1,32,128]{2,1,0:T(8,128)S(1)}, f32[1,32,128]{2,1,0:T(8,128)S(1)}, u32[]{:S(2)}, u32[]{:S(2)}) collective-permute-start(f32[1,32,128]{2,1,0:T(8,128)S(1)} %get-tuple-element.197), channel_id=1, source_target_pairs={{0,32},{32,64},{64,96},{96,128},{128,160},{160,192},{192,224},{224... | collective-permute-start | bytes 49160 | tf_op jit(solution)/shard_map/ppermute | solution.py:19
  92.8 4.3 %collective-permute-done.17 = f32[1,32,128]{2,1,0:T(8,128)S(1)} collective-permute-done((f32[1,32,128]{2,1,0:T(8,128)S(1)}, f32[1,32,128]{2,1,0:T(8,128)S(1)}, u32[]{:S(2)}, u32[]{:S(2)}) %collective-permute-start.17) | collective-permute-done | bytes 16416 | tf_op jit(solution)/shard_map/ppermute | solution.py:20
  97.1 5.4 %collective-permute-start.18 = (f32[34,1,128]{2,1,0:T(1,128)S(1)}, f32[34,1,128]{2,1,0:T(1,128)S(1)}, u32[]{:S(2)}, u32[]{:S(2)}) collective-permute-start(f32[34,1,128]{2,1,0:T(1,128)S(1)} %get-tuple-element.107), channel_id=1, source_target_pairs={{0,1},{1,2},{2,3},{3,4},{4,5},{5,6},{6,7},{7,8},{8,9},{9,10},{10,1... | collective-permute-start | bytes 52232 | tf_op jit(solution)/shard_map/ppermute | solution.py:19
  102.5 1.9 collective-permute-start.19
  107.9 11.1 %all-to-all-start = ((f32[32,32,128]{2,1,0:T(8,128)}), f32[32,32,128]{2,1,0:T(8,128)S(1)}, u32[]{:S(2)}, u32[]{:S(2)}) async-start(f32[32,32,128]{2,1,0:T(8,128)} %fusion.11), calls=%async_computation | async-start | bytes 1048576 | tf_op jit(solution)/shard_map/all_to_all | solution.py:110
  120.3 8.3 %all-to-all-done = f32[32,32,128]{2,1,0:T(8,128)S(1)} async-done(((f32[32,32,128]{2,1,0:T(8,128)}), f32[32,32,128]{2,1,0:T(8,128)S(1)}, u32[]{:S(2)}, u32[]{:S(2)}) %all-to-all-start) | async-done | bytes 524320 | tf_op jit(solution)/shard_map/all_to_all | solution.py:110
  139.0 5.5 %all-to-all-start.2 = ((f32[1,1024,128]{2,0,1:T(1,128)}), f32[1,1024,128]{2,0,1:T(1,128)S(1)}, u32[]{:S(2)}, u32[]{:S(2)}) async-start(f32[1,1024,128]{2,0,1:T(1,128)} %bitcast.8), calls=%async_computation.2 | async-start | bytes 1048576 | tf_op jit(solution)/shard_map/all_to_all | solution.py:92
  145.8 8.4 %all-to-all-done.2 = f32[1,1024,128]{2,0,1:T(1,128)S(1)} async-done(((f32[1,1024,128]{2,0,1:T(1,128)}), f32[1,1024,128]{2,0,1:T(1,128)S(1)}, u32[]{:S(2)}, u32[]{:S(2)}) %all-to-all-start.2) | async-done | bytes 524320 | tf_op jit(solution)/shard_map/all_to_all | solution.py:92
  165.0 6.2 %collective-permute-done.20 = f32[3,32,128]{2,1,0:T(8,128)S(1)} collective-permute-done((f32[3,32,128]{2,1,0:T(8,128)S(1)}, f32[3,32,128]{2,1,0:T(8,128)S(1)}, u32[]{:S(2)}, u32[]{:S(2)}) %collective-permute-start.20) | collective-permute-done | bytes 49184 | tf_op jit(solution)/shard_map/ppermute | solution.py:28
  171.9 70.1 %all-gather.3.cloned.1.call-done = f32[64,32,128]{2,1,0:T(8,128)} async-done(((f32[4,32,128]{2,1,0:T(8,128)}), f32[64,32,128]{2,1,0:T(8,128)}) %all-gather.3.cloned.1.call-update) | async-done | bytes 1048592 | tf_op jit(solution)/shard_map/all_gather | solution.py:150
  242.1 1.9 slice_bitcast_fusion.11
  (219 shorter events, 42.4 us)
Async XLA Ops:
  6.5 11.9 %copy-start.5 = (f32[32,32,128]{2,1,0:T(8,128)S(1)}, f32[32,32,128]{2,1,0:T(8,128)}, u32[]{:S(2)}) copy-start(f32[32,32,128]{2,1,0:T(8,128)} %param.4) | copy-start | bytes 1572868
  6.5 22.5 %copy-start.2 = (f32[32,32,128]{2,1,0:T(8,128)S(1)}, f32[32,32,128]{2,1,0:T(8,128)}, u32[]{:S(2)}) copy-start(f32[32,32,128]{2,1,0:T(8,128)} %param.5) | copy-start | bytes 1572868
  6.5 22.5 %copy-start.1 = (f32[32,32,128]{2,1,0:T(8,128)S(1)}, f32[32,32,128]{2,1,0:T(8,128)}, u32[]{:S(2)}) copy-start(f32[32,32,128]{2,1,0:T(8,128)} %param.6) | copy-start | bytes 1572868
  7.4 11.1 %collective-permute-start.4 = (f32[1,32,128]{2,1,0:T(8,128)S(1)}, f32[1,32,128]{2,1,0:T(8,128)S(1)}, u32[]{:S(2)}, u32[]{:S(2)}) collective-permute-start(f32[1,32,128]{2,1,0:T(8,128)S(1)} %get-tuple-element.204), channel_id=1, source_target_pairs={{0,32},{32,64},{64,96},{96,128},{128,160},{160,192},{192,224},{224... | collective-permute-start | bytes 49160 | tf_op jit(solution)/shard_map/ppermute | solution.py:19
  12.0 17.0 %collective-permute-start = (f32[3,1,32,128]{3,2,1,0:T(8,128)S(1)}, f32[3,1,32,128]{3,2,1,0:T(8,128)S(1)}, u32[]{:S(2)}, u32[]{:S(2)}) collective-permute-start(f32[3,1,32,128]{3,2,1,0:T(8,128)S(1)} %get-tuple-element.65), channel_id=1, source_target_pairs={{0,32},{32,64},{64,96},{96,128},{128,160},{160,192},{192,224},{224... | collective-permute-start | bytes 147464 | tf_op jit(solution)/shard_map/ppermute | solution.py:19
  15.9 13.2 %collective-permute-start.1 = (f32[3,1,32,128]{3,2,1,0:T(8,128)S(1)}, f32[3,1,32,128]{3,2,1,0:T(8,128)S(1)}, u32[]{:S(2)}, u32[]{:S(2)}) collective-permute-start(f32[3,1,32,128]{3,2,1,0:T(8,128)S(1)} %get-tuple-element.66), channel_id=1, source_target_pairs={{32,0},{64,32},{96,64},{128,96},{160,128},{192,160},{224,192},{256... | collective-permute-start | bytes 147464 | tf_op jit(solution)/shard_map/ppermute | solution.py:20
  17.2 6.3 %collective-permute-start.5 = (f32[1,32,128]{2,1,0:T(8,128)S(1)}, f32[1,32,128]{2,1,0:T(8,128)S(1)}, u32[]{:S(2)}, u32[]{:S(2)}) collective-permute-start(f32[1,32,128]{2,1,0:T(8,128)S(1)} %get-tuple-element.203), channel_id=1, source_target_pairs={{32,0},{64,32},{96,64},{128,96},{160,128},{192,160},{224,192},{256... | collective-permute-start | bytes 49160 | tf_op jit(solution)/shard_map/ppermute | solution.py:20
  23.5 12.3 %collective-permute-start.6 = (f32[34,1,128]{2,1,0:T(1,128)S(1)}, f32[34,1,128]{2,1,0:T(1,128)S(1)}, u32[]{:S(2)}, u32[]{:S(2)}) collective-permute-start(f32[34,1,128]{2,1,0:T(1,128)S(1)} %get-tuple-element.113), channel_id=1, source_target_pairs={{0,1},{1,2},{2,3},{3,4},{4,5},{5,6},{6,7},{7,8},{8,9},{9,10},{10,1... | collective-permute-start | bytes 52232 | tf_op jit(solution)/shard_map/ppermute | solution.py:19
  25.4 10.3 %collective-permute-start.7 = (f32[34,1,128]{2,1,0:T(1,128)S(1)}, f32[34,1,128]{2,1,0:T(1,128)S(1)}, u32[]{:S(2)}, u32[]{:S(2)}) collective-permute-start(f32[34,1,128]{2,1,0:T(1,128)S(1)} %get-tuple-element.114), channel_id=1, source_target_pairs={{1,0},{2,1},{3,2},{4,3},{5,4},{6,5},{7,6},{8,7},{9,8},{10,9},{11,1... | collective-permute-start | bytes 52232 | tf_op jit(solution)/shard_map/ppermute | solution.py:20
  30.1 5.7 %collective-permute-start.2 = (f32[3,34,1,128]{3,2,1,0:T(1,128)S(1)}, f32[3,34,1,128]{3,2,1,0:T(1,128)S(1)}, u32[]{:S(2)}, u32[]{:S(2)}) collective-permute-start(f32[3,34,1,128]{3,2,1,0:T(1,128)S(1)} %get-tuple-element.61), channel_id=1, source_target_pairs={{0,1},{1,2},{2,3},{3,4},{4,5},{5,6},{6,7},{7,8},{8,9},{9,10},{10,1... | collective-permute-start | bytes 156680 | tf_op jit(solution)/shard_map/ppermute | solution.py:19
  32.1 6.0 %collective-permute-start.3 = (f32[3,34,1,128]{3,2,1,0:T(1,128)S(1)}, f32[3,34,1,128]{3,2,1,0:T(1,128)S(1)}, u32[]{:S(2)}, u32[]{:S(2)}) collective-permute-start(f32[3,34,1,128]{3,2,1,0:T(1,128)S(1)} %get-tuple-element.62), channel_id=1, source_target_pairs={{1,0},{2,1},{3,2},{4,3},{5,4},{6,5},{7,6},{8,7},{9,8},{10,9},{11,1... | collective-permute-start | bytes 156680 | tf_op jit(solution)/shard_map/ppermute | solution.py:20
  40.5 17.3 %collective-permute-start.8 = (f32[1,32,128]{2,1,0:T(8,128)S(1)}, f32[1,32,128]{2,1,0:T(8,128)S(1)}, u32[]{:S(2)}, u32[]{:S(2)}) collective-permute-start(f32[1,32,128]{2,1,0:T(8,128)S(1)} %get-tuple-element.201), channel_id=1, source_target_pairs={{0,32},{32,64},{64,96},{96,128},{128,160},{160,192},{192,224},{224... | collective-permute-start | bytes 49160 | tf_op jit(solution)/shard_map/ppermute | solution.py:19
  45.5 12.4 %collective-permute-start.9 = (f32[1,32,128]{2,1,0:T(8,128)S(1)}, f32[1,32,128]{2,1,0:T(8,128)S(1)}, u32[]{:S(2)}, u32[]{:S(2)}) collective-permute-start(f32[1,32,128]{2,1,0:T(8,128)S(1)} %get-tuple-element.202), channel_id=1, source_target_pairs={{32,0},{64,32},{96,64},{128,96},{160,128},{192,160},{224,192},{256... | collective-permute-start | bytes 49160 | tf_op jit(solution)/shard_map/ppermute | solution.py:20
  46.8 61.2 %all-to-all-start.1 = ((f32[32,32,128]{2,1,0:T(8,128)}), f32[32,32,128]{2,1,0:T(8,128)S(1)}, u32[]{:S(2)}, u32[]{:S(2)}) async-start(f32[32,32,128]{2,1,0:T(8,128)} %param.7), calls=%async_computation.1 | async-start | bytes 1048576 | tf_op jit(solution)/shard_map/all_to_all | solution.py:111
  57.9 6.9 %collective-permute-start.10 = (f32[34,1,128]{2,1,0:T(1,128)S(1)}, f32[34,1,128]{2,1,0:T(1,128)S(1)}, u32[]{:S(2)}, u32[]{:S(2)}) collective-permute-start(f32[34,1,128]{2,1,0:T(1,128)S(1)} %get-tuple-element.111), channel_id=1, source_target_pairs={{0,1},{1,2},{2,3},{3,4},{4,5},{5,6},{6,7},{7,8},{8,9},{9,10},{10,1... | collective-permute-start | bytes 52232 | tf_op jit(solution)/shard_map/ppermute | solution.py:19
  59.9 5.0 %collective-permute-start.11 = (f32[34,1,128]{2,1,0:T(1,128)S(1)}, f32[34,1,128]{2,1,0:T(1,128)S(1)}, u32[]{:S(2)}, u32[]{:S(2)}) collective-permute-start(f32[34,1,128]{2,1,0:T(1,128)S(1)} %get-tuple-element.112), channel_id=1, source_target_pairs={{1,0},{2,1},{3,2},{4,3},{5,4},{6,5},{7,6},{8,7},{9,8},{10,9},{11,1... | collective-permute-start | bytes 52232 | tf_op jit(solution)/shard_map/ppermute | solution.py:20
  64.8 19.9 %copy-start.3 = (f32[31,32,128]{2,1,0:T(8,128)}, f32[31,32,128]{2,1,0:T(8,128)S(1)}, u32[]{:S(2)}) copy-start(f32[31,32,128]{2,1,0:T(8,128)S(1)} %add_multiply_fusion) | copy-start | bytes 1523716
  65.8 6.0 %collective-permute-start.12 = (f32[1,32,128]{2,1,0:T(8,128)S(1)}, f32[1,32,128]{2,1,0:T(8,128)S(1)}, u32[]{:S(2)}, u32[]{:S(2)}) collective-permute-start(f32[1,32,128]{2,1,0:T(8,128)S(1)} %get-tuple-element.199), channel_id=1, source_target_pairs={{0,32},{32,64},{64,96},{96,128},{128,160},{160,192},{192,224},{224... | collective-permute-start | bytes 49160 | tf_op jit(solution)/shard_map/ppermute | solution.py:19
  70.4 6.8 %collective-permute-start.13 = (f32[1,32,128]{2,1,0:T(8,128)S(1)}, f32[1,32,128]{2,1,0:T(8,128)S(1)}, u32[]{:S(2)}, u32[]{:S(2)}) collective-permute-start(f32[1,32,128]{2,1,0:T(8,128)S(1)} %get-tuple-element.200), channel_id=1, source_target_pairs={{32,0},{64,32},{96,64},{128,96},{160,128},{192,160},{224,192},{256... | collective-permute-start | bytes 49160 | tf_op jit(solution)/shard_map/ppermute | solution.py:20
  77.3 7.4 %collective-permute-start.14 = (f32[34,1,128]{2,1,0:T(1,128)S(1)}, f32[34,1,128]{2,1,0:T(1,128)S(1)}, u32[]{:S(2)}, u32[]{:S(2)}) collective-permute-start(f32[34,1,128]{2,1,0:T(1,128)S(1)} %get-tuple-element.109), channel_id=1, source_target_pairs={{0,1},{1,2},{2,3},{3,4},{4,5},{5,6},{6,7},{7,8},{8,9},{9,10},{10,1... | collective-permute-start | bytes 52232 | tf_op jit(solution)/shard_map/ppermute | solution.py:19
  81.7 4.1 %collective-permute-start.15 = (f32[34,1,128]{2,1,0:T(1,128)S(1)}, f32[34,1,128]{2,1,0:T(1,128)S(1)}, u32[]{:S(2)}, u32[]{:S(2)}) collective-permute-start(f32[34,1,128]{2,1,0:T(1,128)S(1)} %get-tuple-element.110), channel_id=1, source_target_pairs={{1,0},{2,1},{3,2},{4,3},{5,4},{6,5},{7,6},{8,7},{9,8},{10,9},{11,1... | collective-permute-start | bytes 52232 | tf_op jit(solution)/shard_map/ppermute | solution.py:20
  86.7 6.1 %collective-permute-start.16 = (f32[1,32,128]{2,1,0:T(8,128)S(1)}, f32[1,32,128]{2,1,0:T(8,128)S(1)}, u32[]{:S(2)}, u32[]{:S(2)}) collective-permute-start(f32[1,32,128]{2,1,0:T(8,128)S(1)} %get-tuple-element.197), channel_id=1, source_target_pairs={{0,32},{32,64},{64,96},{96,128},{128,160},{160,192},{192,224},{224... | collective-permute-start | bytes 49160 | tf_op jit(solution)/shard_map/ppermute | solution.py:19
  90.6 6.5 %collective-permute-start.17 = (f32[1,32,128]{2,1,0:T(8,128)S(1)}, f32[1,32,128]{2,1,0:T(8,128)S(1)}, u32[]{:S(2)}, u32[]{:S(2)}) collective-permute-start(f32[1,32,128]{2,1,0:T(8,128)S(1)} %get-tuple-element.198), channel_id=1, source_target_pairs={{32,0},{64,32},{96,64},{128,96},{160,128},{192,160},{224,192},{256... | collective-permute-start | bytes 49160 | tf_op jit(solution)/shard_map/ppermute | solution.py:20
  97.1 8.0 %collective-permute-start.18 = (f32[34,1,128]{2,1,0:T(1,128)S(1)}, f32[34,1,128]{2,1,0:T(1,128)S(1)}, u32[]{:S(2)}, u32[]{:S(2)}) collective-permute-start(f32[34,1,128]{2,1,0:T(1,128)S(1)} %get-tuple-element.107), channel_id=1, source_target_pairs={{0,1},{1,2},{2,3},{3,4},{4,5},{5,6},{6,7},{7,8},{8,9},{9,10},{10,1... | collective-permute-start | bytes 52232 | tf_op jit(solution)/shard_map/ppermute | solution.py:19
  102.5 3.8 %collective-permute-start.19 = (f32[34,1,128]{2,1,0:T(1,128)S(1)}, f32[34,1,128]{2,1,0:T(1,128)S(1)}, u32[]{:S(2)}, u32[]{:S(2)}) collective-permute-start(f32[34,1,128]{2,1,0:T(1,128)S(1)} %get-tuple-element.108), channel_id=1, source_target_pairs={{1,0},{2,1},{3,2},{4,3},{5,4},{6,5},{7,6},{8,7},{9,8},{10,9},{11,1... | collective-permute-start | bytes 52232 | tf_op jit(solution)/shard_map/ppermute | solution.py:20
  107.9 20.7 %all-to-all-start = ((f32[32,32,128]{2,1,0:T(8,128)}), f32[32,32,128]{2,1,0:T(8,128)S(1)}, u32[]{:S(2)}, u32[]{:S(2)}) async-start(f32[32,32,128]{2,1,0:T(8,128)} %fusion.11), calls=%async_computation | async-start | bytes 1048576 | tf_op jit(solution)/shard_map/all_to_all | solution.py:110
  137.9 6.9 %copy-start.4 = (f32[31,32,128]{2,1,0:T(8,128)S(1)}, f32[31,32,128]{2,1,0:T(8,128)}, u32[]{:S(2)}) copy-start(f32[31,32,128]{2,1,0:T(8,128)} %copy-done.3) | copy-start | bytes 1523716
  139.0 15.2 %all-to-all-start.2 = ((f32[1,1024,128]{2,0,1:T(1,128)}), f32[1,1024,128]{2,0,1:T(1,128)S(1)}, u32[]{:S(2)}, u32[]{:S(2)}) async-start(f32[1,1024,128]{2,0,1:T(1,128)} %bitcast.8), calls=%async_computation.2 | async-start | bytes 1048576 | tf_op jit(solution)/shard_map/all_to_all | solution.py:92
  144.5 97.5 %all-gather.3.cloned.1.call-start = ((), (), s32[]{:S(2)}) async-start(), calls=%async_computation.3 | async-start | bytes 1114112 | tf_op jit(solution)/shard_map/all_gather | solution.py:150
  163.2 8.1 %copy-start.6 = (f32[31,32,128]{2,1,0:T(8,128)}, f32[31,32,128]{2,1,0:T(8,128)S(1)}, u32[]{:S(2)}) copy-start(f32[31,32,128]{2,1,0:T(8,128)S(1)} %get-tuple-element.60) | copy-start | bytes 1523716
  163.7 7.5 %collective-permute-start.20 = (f32[3,32,128]{2,1,0:T(8,128)S(1)}, f32[3,32,128]{2,1,0:T(8,128)S(1)}, u32[]{:S(2)}, u32[]{:S(2)}) collective-permute-start(f32[3,32,128]{2,1,0:T(8,128)S(1)} %pad_maximum_fusion.15), channel_id=1, source_target_pairs={{32,0},{64,32},{96,64},{128,96},{160,128},{192,160},{224,192},{256... | collective-permute-start | bytes 147464 | tf_op jit(solution)/shard_map/ppermute | solution.py:28
  242.1 2.0 copy-start
  (7 other events, 7.8 us)
Sparse Core Ops, SparseCore 0:
  172.0 69.9 all-gather.2
where the time goes:
time: 256 us; the launch traced here: 255 us
  waiting for transfers between devices  112 us (44%)
  starting transfers between devices  87 us (34%)
  other arithmetic  24.4 us (10%)
  local copies, waits for them, and re-layouts  16.1 us (6%)
  between operations  14.8 us (6%)
    all_gather x1, waiting for transfers between devices, local(): collected = lax.all_gather(equations[None], 'gz', axis=0, tiled=True)  70.1 us
    ppermute x10, starting transfers between devices, padded_2(): before = lax.ppermute(last, axis, up)  36.7 us
    ppermute x10, starting transfers between devices, padded_2(): after = lax.ppermute(leading, axis, down)  21.1 us
    ppermute x10, waiting for transfers between devices, padded_2(): after = lax.ppermute(leading, axis, down)  19.1 us
    all_to_all x1, starting transfers between devices, local(): lax.all_to_all(kappa, 'gy', split_axis=0, concat_axis=1, tiled=True)  11.1 us
    all_to_all x1, starting transfers between devices, local(): lax.all_to_all(state, 'gy', split_axis=0, concat_axis=1, tiled=True)  11.1 us
    all_to_all x1, waiting for transfers between devices, solve_rows(): return lax.all_to_all(solved, 'gy', split_axis=1, concat_axis=0, tiled=True)  8.37 us
    all_to_all x1, waiting for transfers between devices, local(): lax.all_to_all(state, 'gy', split_axis=0, concat_axis=1, tiled=True)  8.34 us
  transfers between devices with their start and end apart: 25, of which 12 were waited for; matrix products, arithmetic and copies ran while one was open for 5% of the time, Pallas kernels for 0%

commit v1 on v0

v1 whole, which is shorter than its diff:
```python
import functools

import jax
import jax.numpy as jnp
from jax import lax
from jax.experimental import pallas as pl
from jax.experimental.pallas import tpu as pltpu
from jax.sharding import PartitionSpec as P

NSUB = 4
RATE = 500.0
HALF_RATE = 250.0
B = 32
X = 128
HZ = 4
HY = 8
C = 8
MESH = pl.DeviceIdType.MESH


def low_rows():
    return lax.broadcasted_iota(jnp.int32, (8, X), 0) < 4


def swap(t):
    return pltpu.roll(t, 4, 0)


def factor(kap, first, last, a_ref, b_ref, inv_ref, lo_ref, hi_ref, tmp_ref):
    e0 = 1.0 + first * kap[0]
    b0 = 1.0 + last * kap[B - 1]
    one = jnp.ones_like(e0)
    inv_ref[0] = e0
    lo_ref[0] = one
    tmp_ref[B - 1] = b0
    hi_ref[B - 1] = one

    def step(s, carry):
        e, eb, ac, bc, kf, kb = carry
        t = B - 1 - s
        kn = kap[s]
        kp = kap[t]
        face = HALF_RATE * (kf + kn)
        a = face / (e + face)
        e = 1.0 + a * e
        ac = ac * a
        faceb = HALF_RATE * (kb + kp)
        b = faceb / (eb + faceb)
        eb = 1.0 + b * eb
        bc = bc * b
        a_ref[s] = a
        inv_ref[s] = e
        lo_ref[s] = ac
        b_ref[t] = b
        tmp_ref[t] = eb
        hi_ref[t] = bc
        return e, eb, ac, bc, kn, kp

    lax.fori_loop(1, B, step, (e0, b0, one, one, kap[0], kap[B - 1]))

    def finish(j, carry):
        inv = 1.0 / (inv_ref[j] + tmp_ref[j] - 1.0)
        inv_ref[j] = inv
        lo_ref[j] = lo_ref[j] * inv
        hi_ref[j] = hi_ref[j] * inv
        return carry

    lax.fori_loop(0, B, finish, 0)


def put_pair(dst, row, first, second):
    low = low_rows()
    for q in range(4):
        f = first[8 * q : 8 * q + 8]
        s = second[8 * q : 8 * q + 8]
        dst[2 * q, row : row + 8] = jnp.where(low, f, swap(s))
        dst[2 * q + 1, row : row + 8] = jnp.where(low, swap(f), s)


def get_pair(src):
    low = low_rows()
    first, second = [], []
    for q in range(4):
        t0 = src[2 * q]
        t1 = src[2 * q + 1]
        first.append(jnp.where(low, t0, swap(t1)))
        second.append(jnp.where(low, swap(t0), t1))
    return jnp.concatenate(first, axis=0), jnp.concatenate(second, axis=0)


def owner_matrix(n, prm, m_ref, y_ref, rf_ref, rb_ref):
    low = low_rows()
    zero = jnp.zeros((8, X), jnp.float32)

    def face(i):
        p = prm[i - 1, 16:24]
        q = prm[i, 16:24]
        k = jnp.where(low, swap(p) + q, p + swap(q))
        return 1.0 / (HALF_RATE * k)

    y_ref[0] = zero
    y_ref[n] = zero
    r0 = prm[0, 0:8]
    rb0 = prm[n - 1, 0:8]
    rf_ref[0] = r0
    rb_ref[n - 1] = rb0
    m_ref[0] = zero
    m_ref[n - 1] = zero

    def step(s, carry):
        r, rb = carry
        z = prm[s, 0:8]
        zt = prm[s, 8:16]
        t = zt / (r + face(s) + swap(z))
        r = z - zt * t
        rf_ref[s] = r
        i = n - 1 - s
        zb = prm[i, 0:8]
        ztb = prm[i, 8:16]
        tb = ztb / (rb + face(i + 1) + swap(zb))
        rb = zb - ztb * tb
        rb_ref[i] = rb
        m_ref[s] = jnp.where(low, m_ref[s], t)
        m_ref[i] = jnp.where(low, tb, m_ref[i])
        return r, rb

    def clear(s, carry):
        m_ref[s] = zero
        return carry

    lax.fori_loop(0, n, clear, 0)
    lax.fori_loop(1, n, step, (r0, rb0))

    def admit(i, carry):
        y_ref[i] = 1.0 / (swap(rf_ref[i - 1]) + face(i) + rb_ref[i])
        return carry

    lax.fori_loop(1, n, admit, 0)


def owner_scan(n, g_ref, m_ref, u_ref, v_ref):
    zero = jnp.zeros((8, X), jnp.float32)
    u_ref[0] = zero
    v_ref[n] = zero

    def step(s, carry):
        u, v = carry
        g = g_ref[s]
        m = m_ref[s]
        u = g - m * swap(g) + m * u
        u_ref[s + 1] = u
        i = n - 1 - s
        gb = g_ref[i]
        mb = m_ref[i]
        v = gb - mb * swap(gb) + mb * v
        v_ref[i] = v
        return u, v

    lax.fori_loop(0, n, step, (zero, zero))


def owner_result(b, u_ref, v_ref, y_ref):
    low = low_rows()
    here = (swap(u_ref[b]) - v_ref[b]) * y_ref[b]
    after = (swap(u_ref[b + 1]) - v_ref[b + 1]) * y_ref[b + 1]
    return jnp.where(low, here, -swap(after))


def local_scan(r_ref, a_ref, b_ref, f_ref, g_ref, inv_ref):
    r0 = r_ref[0]
    rb0 = r_ref[B - 1]
    f_ref[0] = r0
    g_ref[B - 1] = jnp.zeros_like(r0)

    def step(s, carry):
        f, g = carry
        t = B - 1 - s
        f = r_ref[s] + a_ref[s] * f
        bg = b_ref[t] * g
        g = r_ref[t] + bg
        f_ref[s] = f
        g_ref[t] = bg
        return f, g

    f, g = lax.fori_loop(1, B, step, (r0, rb0))
    return g * inv_ref[0], f * inv_ref[B - 1]


def kernel(nz, ny, *refs):
    (c_hbm, v_hbm, w_hbm, k_hbm, o_hbm,
     ca, cb, vv, ww, kz, ky, k0, cym, cyp, czm, czp,
     ay, by, iy, ly, hy, az, bz, iz, lz, hz, tmp, rr, ff, gg, uz, out,
     psy, psz, pry, prz, gsy, gsz, gry, grz,
     my, yy, uy, vy, mz, yz, uo, vo, rf, rb,
     rsy, rsz, rety, retz,
     lsem, hsend, hrecv, psem, grsem, rtsem) = refs
    p = lax.axis_index("gz")
    g = lax.axis_index("gy")

    def zi(k):
        return lax.rem(p + k + nz, nz)

    def yi(k):
        return lax.rem(g + k + ny, ny)

    bar = pltpu.get_barrier_semaphore()

    def greet(pz, gy):
        pl.semaphore_signal(bar, inc=1, device_id=(pz, gy), device_id_type=MESH)

    for dz in (1, -1):
        for dy in (1, -1):
            greet(zi(dz), yi(dy))
    for k in range(1, nz):
        greet(zi(k), g)
    for k in range(1, ny):
        greet(p, yi(k))

    loads = [
        pltpu.make_async_copy(k_hbm, kz, lsem.at[0]),
        pltpu.make_async_copy(c_hbm, ca.at[HZ : HZ + B, HY : HY + B], lsem.at[1]),
        pltpu.make_async_copy(v_hbm, vv.at[HZ : HZ + B, HY : HY + B], lsem.at[2]),
        pltpu.make_async_copy(w_hbm, ww.at[HZ : HZ + B, HY : HY + B], lsem.at[3]),
    ]
    for ld in loads:
        ld.start()

    pl.semaphore_wait(bar, 4 + (nz - 1) + (ny - 1))

    zsrc = {1: slice(B - HZ, B), 0: slice(0, B), -1: slice(0, HZ)}
    zdst = {1: slice(0, HZ), 0: slice(HZ, HZ + B), -1: slice(HZ + B, 2 * HZ + B)}
    ysrc = {1: slice(B - HY, B), 0: slice(0, B), -1: slice(0, HY)}
    ydst = {1: slice(0, HY), 0: slice(HY, HY + B), -1: slice(HY + B, 2 * HY + B)}
    halo = []
    for dz, dy in ((1, 0), (-1, 0), (0, 1), (0, -1), (1, 1), (1, -1), (-1, 1), (-1, -1)):
        for src, dst in ((c_hbm, ca), (v_hbm, vv), (w_hbm, ww)):
            i = len(halo)
            halo.append(pltpu.make_async_remote_copy(
                src.at[zsrc[dz], ysrc[dy]], dst.at[zdst[dz], ydst[dy]],
                hsend.at[i], hrecv.at[i],
                device_id=(zi(dz), yi(dy)), device_id_type=MESH))
    for h in halo:
        h.start()

    loads[0].wait()
    kflat = kz.reshape(B * B, X)

    def turn(j, carry):
        ky[j] = kflat[pl.ds(j, B, stride=B), :]
        return carry

    lax.fori_loop(0, B, turn, 0)
    yfirst = jnp.where(g == 0, RATE, 0.0).astype(jnp.float32)
    ylast = jnp.where(g == ny - 1, RATE, 0.0).astype(jnp.float32)
    zfirst = jnp.where(p == 0, RATE, 0.0).astype(jnp.float32)
    zlast = jnp.where(p == nz - 1, RATE, 0.0).astype(jnp.float32)

    factor(ky, yfirst, ylast, ay, by, iy, ly, hy, tmp)
    put_pair(psy, 0, ly[0], hy[B - 1])
    put_pair(psy, 8, hy[0], hy[0])
    put_pair(psy, 16, ky[0], ky[B - 1])
    pry[g] = psy[lax.rem(g, C)]

    def to_y(src, dst, sem, k):
        return pltpu.make_async_remote_copy(
            src.at[lax.rem(g + k, C)], dst.at[g], sem.at[0], sem.at[1],
            device_id=(p, yi(k)), device_id_type=MESH)

    def to_z(src, dst, sem, k):
        return pltpu.make_async_remote_copy(
            src.at[lax.rem(p + k, C)], dst.at[p], sem.at[0], sem.at[1],
            device_id=(zi(k), g), device_id_type=MESH)

    def wait_all(ref, count, sem):
        part = ref.at[pl.ds(0, count)]
        pltpu.make_async_copy(part, part, sem).wait()

    for k in range(1, ny):
        to_y(psy, pry, psem.at[0], k).start()

    factor(kz, zfirst, zlast, az, bz, iz, lz, hz, tmp)
    put_pair(psz, 0, lz[0], hz[B - 1])
    put_pair(psz, 8, hz[0], hz[0])
    put_pair(psz, 16, kz[0], kz[B - 1])
    prz[p] = psz[lax.rem(p, C)]
    for k in range(1, nz):
        to_z(psz, prz, psem.at[1], k).start()

    for ld in loads[1:]:
        ld.wait()
    for h in halo:
        h.wait_recv()

    zero3 = jnp.zeros((HZ, B + 2 * HY, X), jnp.float32)
    zero_row = jnp.zeros((HY, X), jnp.float32)

    def zero_y(at):
        def body(z, carry):
            for ref in (ca, vv, ww):
                ref[z, at : at + HY] = zero_row
            return carry

        lax.fori_loop(0, B + 2 * HZ, body, 0)

    @pl.when(p == 0)
    def _():
        for ref in (ca, vv, ww):
            ref[0:HZ] = zero3

    @pl.when(p == nz - 1)
    def _():
        for ref in (ca, vv, ww):
            ref[HZ + B : 2 * HZ + B] = zero3

    @pl.when(g == 0)
    def _():
        zero_y(0)

    @pl.when(g == ny - 1)
    def _():
        zero_y(HY + B)

    LO, N5 = 4, B + 8

    def weights(z, carry):
        vc = vv[z, LO : LO + N5]
        vm = vv[z, LO - 1 : LO - 1 + N5]
        vp = vv[z, LO + 1 : LO + 1 + N5]
        wc = ww[z, LO : LO + N5]
        wm = ww[z - 1, LO : LO + N5]
        wp = ww[z + 1, LO : LO + N5]
        fyp = 0.5 * (vc + vp)
        fym = 0.5 * (vm + vc)
        fzp = 0.5 * (wc + wp)
        fzm = 0.5 * (wm + wc)
        cyp[z] = -jnp.minimum(fyp, 0.0)
        cym[z] = jnp.maximum(fym, 0.0)
        czp[z] = -jnp.minimum(fzp, 0.0)
        czm[z] = jnp.maximum(fzm, 0.0)
        k0[z] = (1.0 - jnp.maximum(fyp, 0.0) + jnp.minimum(fym, 0.0)
                 - jnp.maximum(fzp, 0.0) + jnp.minimum(fzm, 0.0))
        return carry

    lax.fori_loop(1, B + 2 * HZ - 1, weights, 0)

    wrefs = (k0, cym, cyp, czm, czp)
    zero_w = jnp.zeros((HZ - 1, N5, X), jnp.float32)

    def zero_wy(at):
        def body(z, carry):
            for ref in wrefs:
                ref[z, at : at + 4] = jnp.zeros((4, X), jnp.float32)
            return carry

        lax.fori_loop(1, B + 2 * HZ - 1, body, 0)

    @pl.when(p == 0)
    def _():
        for ref in wrefs:
            ref[1:HZ] = zero_w

    @pl.when(p == nz - 1)
    def _():
        for ref in wrefs:
            ref[HZ + B : 2 * HZ + B - 1] = zero_w

    @pl.when(g == 0)
    def _():
        zero_wy(0)

    @pl.when(g == ny - 1)
    def _():
        zero_wy(4 + B)

    for s in range(1, NSUB + 1):
        src, dst = (ca, cb) if s % 2 == 1 else (cb, ca)

        def sub(z, carry, src=src, dst=dst):
            new = (k0[z] * src[z, LO : LO + N5]
                   + cym[z] * src[z, LO - 1 : LO - 1 + N5]
                   + cyp[z] * src[z, LO + 1 : LO + 1 + N5]
                   + czm[z] * src[z - 1, LO : LO + N5]
                   + czp[z] * src[z + 1, LO : LO + N5])
            dst[z, LO : LO + N5] = new
            return carry

        lax.fori_loop(s, B + 2 * HZ - s, sub, 0)

    cflat = ca.reshape((B + 2 * HZ) * (B + 2 * HY), X)

    def turn_r(j, carry):
        rr[j] = cflat[pl.ds(HZ * (B + 2 * HY) + HY + j, B, stride=B + 2 * HY), :]
        return carry

    lax.fori_loop(0, B, turn_r, 0)
    g0, gl = local_scan(rr, ay, by, ff, gg, iy)
    put_pair(gsy, 0, g0, gl)
    gry[g] = gsy[lax.rem(g, C)]
    for k in range(1, ny):
        to_y(gsy, gry, grsem.at[0], k).start()

    wait_all(pry, ny - 1, psem.at[0, 1])
    owner_matrix(ny, pry, my, yy, rf, rb)

    def base(j, carry):
        ff[j] = (ff[j] + gg[j]) * inv_now[j]
        return carry

    inv_now = iy
    lax.fori_loop(0, B, base, 0)

    wait_all(gry, ny - 1, grsem.at[0, 1])
    owner_scan(ny, gry, my, uy, vy)
    yc = lax.rem(g, C)
    yb = g - yc
    rety[yc] = owner_result(g, uy, vy, yy)
    for m in range(1, C):
        b = yb + lax.rem(yc + m, C)
        rsy[m] = owner_result(b, uy, vy, yy)
        pltpu.make_async_remote_copy(
            rsy.at[m], rety.at[yc], rtsem.at[0, 0], rtsem.at[0, 1],
            device_id=(p, b), device_id_type=MESH).start()

    wait_all(prz, nz - 1, psem.at[1, 1])
    owner_matrix(nz, prz, mz, yz, rf, rb)

    wait_all(rety, C - 1, rtsem.at[0, 1])
    flo, fhi = get_pair(rety)
    uflat = uz.reshape(B * B, X)

    def end_y(j, carry):
        uflat[pl.ds(j, B, stride=B), :] = ff[j] + flo * ly[j] + fhi * hy[j]
        return carry

    lax.fori_loop(0, B, end_y, 0)

    g0, gl = local_scan(uz, az, bz, ff, gg, iz)
    put_pair(gsz, 0, g0, gl)
    grz[p] = gsz[lax.rem(p, C)]
    for k in range(1, nz):
        to_z(gsz, grz, grsem.at[1], k).start()
    inv_now = iz

    def base_z(j, carry):
        ff[j] = (ff[j] + gg[j]) * iz[j]
        return carry

    lax.fori_loop(0, B, base_z, 0)
    wait_all(grz, nz - 1, grsem.at[1, 1])
    owner_scan(nz, grz, mz, uo, vo)
    zc = lax.rem(p, C)
    retz[zc] = owner_result(p, uo, vo, yz)
    others = [o for o in range(-(C // 2), C // 2) if o != 0]
    for m, o in enumerate(others):
        b = zi(o)
        rsz[m] = owner_result(b, uo, vo, yz)
        pltpu.make_async_remote_copy(
            rsz.at[m], retz.at[zc], rtsem.at[1, 0], rtsem.at[1, 1],
            device_id=(b, g), device_id_type=MESH).start()
    wait_all(retz, C - 1, rtsem.at[1, 1])
    flo, fhi = get_pair(retz)

    def end_z(j, carry):
        out[j] = ff[j] + flo * lz[j] + fhi * hz[j]
        return carry

    lax.fori_loop(0, B, end_z, 0)
    store = pltpu.make_async_copy(out, o_hbm, lsem.at[4])
    store.start()
    for h in halo:
        h.wait_send()
    wait_all(pry, ny - 1, psem.at[0, 0])
    wait_all(prz, nz - 1, psem.at[1, 0])
    wait_all(gry, ny - 1, grsem.at[0, 0])
    wait_all(grz, nz - 1, grsem.at[1, 0])
    wait_all(rety, C - 1, rtsem.at[0, 0])
    wait_all(retz, C - 1, rtsem.at[1, 0])
    store.wait()


def local(nz, ny, tracer, y_speed, z_speed, kappa):
    f32 = jnp.float32
    pad = pltpu.VMEM((B + 2 * HZ, B + 2 * HY, X), f32)
    blk = pltpu.VMEM((B, B, X), f32)
    wgt = pltpu.VMEM((B + 2 * HZ, B + 8, X), f32)

    def tiles(n, rows=8):
        return pltpu.VMEM((n, rows, X), f32)

    scratch = (
        [pad] * 4 + [blk] * 2 + [wgt] * 5
        + [blk] * 5 + [blk] * 5 + [blk] * 6
        + [tiles(C, 24), tiles(C, 24), tiles(ny, 24), tiles(nz, 24)]
        + [tiles(C), tiles(C), tiles(ny), tiles(nz)]
        + [tiles(ny), tiles(ny + 1), tiles(ny + 1), tiles(ny + 1)]
        + [tiles(nz), tiles(nz + 1), tiles(nz + 1), tiles(nz + 1)]
        + [tiles(ny), tiles(ny)]
        + [tiles(C), tiles(C), tiles(C), tiles(C)]
        + [pltpu.SemaphoreType.DMA((5,)), pltpu.SemaphoreType.DMA((24,)),
           pltpu.SemaphoreType.DMA((24,)), pltpu.SemaphoreType.DMA((2, 2)),
           pltpu.SemaphoreType.DMA((2, 2)), pltpu.SemaphoreType.DMA((2, 2))]
    )
    return pl.pallas_call(
        functools.partial(kernel, nz, ny),
        out_shape=jax.ShapeDtypeStruct(tracer.shape, f32),
        in_specs=[pl.BlockSpec(memory_space=pl.ANY)] * 4,
        out_specs=pl.BlockSpec(memory_space=pl.ANY),
        scratch_shapes=scratch,
        compiler_params=pltpu.CompilerParams(
            collective_id=0, has_side_effects=True, vmem_limit_bytes=48 * 1024 * 1024),
    )(tracer, y_speed, z_speed, kappa)


def solution(mesh):
    nz, ny = mesh.shape["gz"], mesh.shape["gy"]
    return jax.shard_map(
        functools.partial(local, nz, ny),
        mesh=mesh,
        in_specs=(P("gz", "gy", None),) * 4,
        out_specs=P("gz", "gy", None),
        check_vma=False,
    )
```

time: 256 us -> 61 us (0.24)
  the two profiles are of different devices: /device:TPU:24 before, /device:TPU:1 now
where the time goes in v1:
time: 61 us; the launch traced here: 60.7 us
  Pallas kernels  55.7 us (91%)
  local copies, waits for them, and re-layouts  4.96 us (8%)
    pallas_call x1, Pallas kernels, local(): pl.pallas_call(functools.partial(kernel, nz, ny), out_shape=jax.ShapeDtyp...  55.7 us
    unnamed x9, local copies, waits for them, and re-layouts  4.96 us

profile of v1, /device:TPU:1, one launch (start us, length us, event | category | flops | bytes accessed | tf_op | source)
XLA Modules:
  0.0 60.7 jit_solution(14501818860578575009)
XLA Ops:
  0.0 0.0 copy-start
  0.0 1.0 %copy-done = f32[32,32,128]{2,1,0:T(8,128)S(1)} copy-done((f32[32,32,128]{2,1,0:T(8,128)S(1)}, f32[32,32,128]{2,1,0:T(8,128)}, u32[]{:S(2)}) %copy-start) | copy-done | bytes 524312
  1.0 0.0 copy-start.1
  1.0 1.0 %copy-done.1 = f32[32,32,128]{2,1,0:T(8,128)S(1)} copy-done((f32[32,32,128]{2,1,0:T(8,128)S(1)}, f32[32,32,128]{2,1,0:T(8,128)}, u32[]{:S(2)}) %copy-start.1) | copy-done | bytes 524312
  2.1 0.0 copy-start.2
  2.1 1.0 %copy-done.2 = f32[32,32,128]{2,1,0:T(8,128)S(1)} copy-done((f32[32,32,128]{2,1,0:T(8,128)S(1)}, f32[32,32,128]{2,1,0:T(8,128)}, u32[]{:S(2)}) %copy-start.2) | copy-done | bytes 524312
  3.1 0.0 copy-start.3
  3.1 1.0 %copy-done.3 = f32[32,32,128]{2,1,0:T(8,128)S(1)} copy-done((f32[32,32,128]{2,1,0:T(8,128)S(1)}, f32[32,32,128]{2,1,0:T(8,128)}, u32[]{:S(2)}) %copy-start.3) | copy-done | bytes 524312
  4.2 55.7 %shard_map.46 = f32[32,32,128]{2,1,0:T(8,128)S(1)} custom-call(f32[32,32,128]{2,1,0:T(8,128)S(1)} %copy-done, f32[32,32,128]{2,1,0:T(8,128)S(1)} %copy-done.1, f32[32,32,128]{2,1,0:T(8,128)S(1)} %copy-done.2, f32[32,32,128]{2,1,0:T(8,128)S(1)} %copy-done.3), custom_call_target="tpu_custom_call" | custom-call | tf_op jit(solution)/shard_map/pallas_call | solution.py:503
  59.9 0.8 %copy.6 = f32[32,32,128]{2,1,0:T(8,128)} copy(f32[32,32,128]{2,1,0:T(8,128)S(1)} %shard_map.46) | data formatting | bytes 1048576
Async XLA Ops:
  0.0 1.0 %copy-start = (f32[32,32,128]{2,1,0:T(8,128)S(1)}, f32[32,32,128]{2,1,0:T(8,128)}, u32[]{:S(2)}) copy-start(f32[32,32,128]{2,1,0:T(8,128)} %refs_0_.1) | copy-start | bytes 1572868
  1.0 1.0 %copy-start.1 = (f32[32,32,128]{2,1,0:T(8,128)S(1)}, f32[32,32,128]{2,1,0:T(8,128)}, u32[]{:S(2)}) copy-start(f32[32,32,128]{2,1,0:T(8,128)} %refs_1_.1) | copy-start | bytes 1572868
  2.1 1.0 %copy-start.2 = (f32[32,32,128]{2,1,0:T(8,128)S(1)}, f32[32,32,128]{2,1,0:T(8,128)}, u32[]{:S(2)}) copy-start(f32[32,32,128]{2,1,0:T(8,128)} %refs_2_.1) | copy-start | bytes 1572868
  3.1 1.0 %copy-start.3 = (f32[32,32,128]{2,1,0:T(8,128)S(1)}, f32[32,32,128]{2,1,0:T(8,128)}, u32[]{:S(2)}) copy-start(f32[32,32,128]{2,1,0:T(8,128)} %refs_3_.1) | copy-start | bytes 1572868

commit v2 on v1

--- a/solution.py
+++ b/solution.py
@@ -227,17 +227,23 @@
 
     pl.semaphore_wait(bar, 4 + (nz - 1) + (ny - 1))
 
-    zsrc = {1: slice(B - HZ, B), 0: slice(0, B), -1: slice(0, HZ)}
-    zdst = {1: slice(0, HZ), 0: slice(HZ, HZ + B), -1: slice(HZ + B, 2 * HZ + B)}
-    ysrc = {1: slice(B - HY, B), 0: slice(0, B), -1: slice(0, HY)}
-    ydst = {1: slice(0, HY), 0: slice(HY, HY + B), -1: slice(HY + B, 2 * HY + B)}
+    def near(d, size, pad, width):
+        if d == 0:
+            return slice(0, size), slice(pad, pad + size)
+        if d > 0:
+            return slice(size - width, size), slice(pad - width, pad)
+        return slice(0, width), slice(pad + size, pad + size + width)
+
     halo = []
-    for dz, dy in ((1, 0), (-1, 0), (0, 1), (0, -1), (1, 1), (1, -1), (-1, 1), (-1, -1)):
-        for src, dst in ((c_hbm, ca), (v_hbm, vv), (w_hbm, ww)):
+    for dz, dy in ((0, 1), (0, -1), (1, 0), (-1, 0), (1, 1), (1, -1), (-1, 1), (-1, -1)):
+        for src, dst, wz, wy in ((c_hbm, ca, 4, 4), (v_hbm, vv, 3, 4), (w_hbm, ww, 4, 3)):
+            if dz and dy:
+                wz, wy = 3, 3
+            zs, zd = near(dz, B, HZ, wz)
+            ys, yd = near(dy, B, HY, wy)
             i = len(halo)
             halo.append(pltpu.make_async_remote_copy(
-                src.at[zsrc[dz], ysrc[dy]], dst.at[zdst[dz], ydst[dy]],
-                hsend.at[i], hrecv.at[i],
+                src.at[zs, ys], dst.at[zd, yd], hsend.at[i], hrecv.at[i],
                 device_id=(zi(dz), yi(dy)), device_id_type=MESH))
     for h in halo:
         h.start()
@@ -283,13 +289,13 @@
     put_pair(psz, 8, hz[0], hz[0])
     put_pair(psz, 16, kz[0], kz[B - 1])
     prz[p] = psz[lax.rem(p, C)]
-    for k in range(1, nz):
-        to_z(psz, prz, psem.at[1], k).start()
 
     for ld in loads[1:]:
         ld.wait()
     for h in halo:
         h.wait_recv()
+    for k in range(1, nz):
+        to_z(psz, prz, psem.at[1], k).start()
 
     zero3 = jnp.zeros((HZ, B + 2 * HY, X), jnp.float32)
     zero_row = jnp.zeros((HY, X), jnp.float32)
@@ -322,26 +328,26 @@
 
     LO, N5 = 4, B + 8
 
+    def z_face(a, b):
+        f = 0.5 * (a + b)
+        return jnp.maximum(f, 0.0), jnp.minimum(f, 0.0)
+
     def weights(z, carry):
+        wc, zm_pos, zm_neg = carry
+        wp = ww[z + 1, LO : LO + N5]
+        zp_pos, zp_neg = z_face(wc, wp)
         vc = vv[z, LO : LO + N5]
-        vm = vv[z, LO - 1 : LO - 1 + N5]
-        vp = vv[z, LO + 1 : LO + 1 + N5]
-        wc = ww[z, LO : LO + N5]
-        wm = ww[z - 1, LO : LO + N5]
-        wp = ww[z + 1, LO : LO + N5]
-        fyp = 0.5 * (vc + vp)
-        fym = 0.5 * (vm + vc)
-        fzp = 0.5 * (wc + wp)
-        fzm = 0.5 * (wm + wc)
-        cyp[z] = -jnp.minimum(fyp, 0.0)
-        cym[z] = jnp.maximum(fym, 0.0)
-        czp[z] = -jnp.minimum(fzp, 0.0)
-        czm[z] = jnp.maximum(fzm, 0.0)
-        k0[z] = (1.0 - jnp.maximum(fyp, 0.0) + jnp.minimum(fym, 0.0)
-                 - jnp.maximum(fzp, 0.0) + jnp.minimum(fzm, 0.0))
-        return carry
-
-    lax.fori_loop(1, B + 2 * HZ - 1, weights, 0)
+        ym_pos, ym_neg = z_face(vv[z, LO - 1 : LO - 1 + N5], vc)
+        yp_pos, yp_neg = z_face(vc, vv[z, LO + 1 : LO + 1 + N5])
+        cyp[z] = yp_neg
+        cym[z] = ym_pos
+        czp[z] = zp_neg
+        czm[z] = zm_pos
+        k0[z] = ((1.0 - yp_pos) + (ym_neg - zp_pos)) + zm_neg
+        return wp, zp_pos, zp_neg
+
+    w1 = ww[1, LO : LO + N5]
+    lax.fori_loop(1, B + 2 * HZ - 1, weights, (w1, *z_face(ww[0, LO : LO + N5], w1)), unroll=2)
 
     wrefs = (k0, cym, cyp, czm, czp)
     zero_w = jnp.zeros((HZ - 1, N5, X), jnp.float32)
@@ -376,11 +382,11 @@
         src, dst = (ca, cb) if s % 2 == 1 else (cb, ca)
 
         def sub(z, carry, src=src, dst=dst):
-            new = (k0[z] * src[z, LO : LO + N5]
-                   + cym[z] * src[z, LO - 1 : LO - 1 + N5]
-                   + cyp[z] * src[z, LO + 1 : LO + 1 + N5]
-                   + czm[z] * src[z - 1, LO : LO + N5]
-                   + czp[z] * src[z + 1, LO : LO + N5])
+            new = ((k0[z] * src[z, LO : LO + N5]
+                    + cym[z] * src[z, LO - 1 : LO - 1 + N5])
+                   - (cyp[z] * src[z, LO + 1 : LO + 1 + N5]
+                      - czm[z] * src[z - 1, LO : LO + N5])
+                   - czp[z] * src[z + 1, LO : LO + N5])
             dst[z, LO : LO + N5] = new
             return carry
 
@@ -507,7 +513,7 @@
         out_specs=pl.BlockSpec(memory_space=pl.ANY),
         scratch_shapes=scratch,
         compiler_params=pltpu.CompilerParams(
-            collective_id=0, has_side_effects=True, vmem_limit_bytes=48 * 1024 * 1024),
+            collective_id=0, has_side_effects=True, vmem_limit_bytes=67043328),
     )(tracer, y_speed, z_speed, kappa)
 
 

time: 61 us -> 54.7 us (0.90)
  the two profiles are of different devices: /device:TPU:1 before, /device:TPU:4 now
where the time goes in v2:
time: 54.7 us; the launch traced here: 54.6 us
  Pallas kernels  52.7 us (96%)
  local copies, waits for them, and re-layouts  1.87 us (3%)
    pallas_call x1, Pallas kernels, local(): pl.pallas_call(functools.partial(kernel, nz, ny), out_shape=jax.ShapeDtyp...  52.7 us
    unnamed x1, local copies, waits for them, and re-layouts  1.87 us

profile of v2, /device:TPU:4, one launch (start us, length us, event | category | flops | bytes accessed | tf_op | source)
XLA Modules:
  0.0 54.6 jit_solution(8221746744660921628)
XLA Ops:
  0.0 52.7 %shard_map.46 = f32[32,32,128]{2,1,0:T(8,128)} custom-call(f32[32,32,128]{2,1,0:T(8,128)} %refs_0_.1, f32[32,32,128]{2,1,0:T(8,128)} %refs_1_.1, f32[32,32,128]{2,1,0:T(8,128)} %refs_2_.1, f32[32,32,128]{2,1,0:T(8,128)} %refs_3_.1), custom_call_target="tpu_custom_call" | custom-call | tf_op jit(solution)/shard_map/pallas_call | solution.py:509
  52.7 1.9 %copy.6 = f32[32,32,128]{2,1,0:T(8,128)} copy(f32[32,32,128]{2,1,0:T(8,128)} %shard_map.46) | data formatting | bytes 1048576

commit v3 on v2

--- a/solution.py
+++ b/solution.py
@@ -15,6 +15,8 @@
 HZ = 4
 HY = 8
 C = 8
+PR = 12
+OUT = 8
 MESH = pl.DeviceIdType.MESH
 
 
@@ -92,11 +94,9 @@
     low = low_rows()
     zero = jnp.zeros((8, X), jnp.float32)
 
-    def face(i):
-        p = prm[i - 1, 16:24]
-        q = prm[i, 16:24]
-        k = jnp.where(low, swap(p) + q, p + swap(q))
-        return 1.0 / (HALF_RATE * k)
+    def block(i):
+        c = prm[i, 8:16]
+        return prm[i, 0:8], jnp.where(low, c, swap(c))
 
     y_ref[0] = zero
     y_ref[n] = zero
@@ -109,15 +109,13 @@
 
     def step(s, carry):
         r, rb = carry
-        z = prm[s, 0:8]
-        zt = prm[s, 8:16]
-        t = zt / (r + face(s) + swap(z))
+        z, zt = block(s)
+        t = zt / (r + swap(z))
         r = z - zt * t
         rf_ref[s] = r
         i = n - 1 - s
-        zb = prm[i, 0:8]
-        ztb = prm[i, 8:16]
-        tb = ztb / (rb + face(i + 1) + swap(zb))
+        zb, ztb = block(i)
+        tb = ztb / (rb + swap(zb))
         rb = zb - ztb * tb
         rb_ref[i] = rb
         m_ref[s] = jnp.where(low, m_ref[s], t)
@@ -132,7 +130,7 @@
     lax.fori_loop(1, n, step, (r0, rb0))
 
     def admit(i, carry):
-        y_ref[i] = 1.0 / (swap(rf_ref[i - 1]) + face(i) + rb_ref[i])
+        y_ref[i] = 1.0 / (swap(rf_ref[i - 1]) + rb_ref[i])
         return carry
 
     lax.fori_loop(1, n, admit, 0)
@@ -193,7 +191,7 @@
      psy, psz, pry, prz, gsy, gsz, gry, grz,
      my, yy, uy, vy, mz, yz, uo, vo, rf, rb,
      rsy, rsz, rety, retz,
-     lsem, hsend, hrecv, psem, grsem, rtsem) = refs
+     kye, kze, lsem, hsend, hrecv, psem, grsem, rtsem, ksem) = refs
     p = lax.axis_index("gz")
     g = lax.axis_index("gy")
 
@@ -245,7 +243,15 @@
             halo.append(pltpu.make_async_remote_copy(
                 src.at[zs, ys], dst.at[zd, yd], hsend.at[i], hrecv.at[i],
                 device_id=(zi(dz), yi(dy)), device_id_type=MESH))
-    for h in halo:
+    edges = [
+        pltpu.make_async_remote_copy(
+            k_hbm.at[:, B - 1 : B], kye.at[:, 0:1], ksem.at[0], ksem.at[1],
+            device_id=(p, yi(1)), device_id_type=MESH),
+        pltpu.make_async_remote_copy(
+            k_hbm.at[B - 1], kze, ksem.at[2], ksem.at[3],
+            device_id=(zi(1), g), device_id_type=MESH),
+    ]
+    for h in edges + halo:
         h.start()
 
     loads[0].wait()
@@ -262,9 +268,10 @@
     zlast = jnp.where(p == nz - 1, RATE, 0.0).astype(jnp.float32)
 
     factor(ky, yfirst, ylast, ay, by, iy, ly, hy, tmp)
-    put_pair(psy, 0, ly[0], hy[B - 1])
+    edges[0].wait_recv()
+    below = kye.reshape(B * 8, X)[pl.ds(0, B, stride=8), :]
+    put_pair(psy, 0, ly[0] + 1.0 / (HALF_RATE * (below + ky[0])), hy[B - 1])
     put_pair(psy, 8, hy[0], hy[0])
-    put_pair(psy, 16, ky[0], ky[B - 1])
     pry[g] = psy[lax.rem(g, C)]
 
     def to_y(src, dst, sem, k):
@@ -282,12 +289,12 @@
         pltpu.make_async_copy(part, part, sem).wait()
 
     for k in range(1, ny):
-        to_y(psy, pry, psem.at[0], k).start()
+        to_y(psy.at[:, 0:PR], pry.at[:, 0:PR], psem.at[0], k).start()
 
     factor(kz, zfirst, zlast, az, bz, iz, lz, hz, tmp)
-    put_pair(psz, 0, lz[0], hz[B - 1])
+    edges[1].wait_recv()
+    put_pair(psz, 0, lz[0] + 1.0 / (HALF_RATE * (kze[...] + kz[0])), hz[B - 1])
     put_pair(psz, 8, hz[0], hz[0])
-    put_pair(psz, 16, kz[0], kz[B - 1])
     prz[p] = psz[lax.rem(p, C)]
 
     for ld in loads[1:]:
@@ -295,7 +302,7 @@
     for h in halo:
         h.wait_recv()
     for k in range(1, nz):
-        to_z(psz, prz, psem.at[1], k).start()
+        to_z(psz.at[:, 0:PR], prz.at[:, 0:PR], psem.at[1], k).start()
 
     zero3 = jnp.zeros((HZ, B + 2 * HY, X), jnp.float32)
     zero_row = jnp.zeros((HY, X), jnp.float32)
@@ -378,7 +385,7 @@
     def _():
         zero_wy(4 + B)
 
-    for s in range(1, NSUB + 1):
+    for s in range(1, NSUB):
         src, dst = (ca, cb) if s % 2 == 1 else (cb, ca)
 
         def sub(z, carry, src=src, dst=dst):
@@ -392,20 +399,28 @@
 
         lax.fori_loop(s, B + 2 * HZ - s, sub, 0)
 
-    cflat = ca.reshape((B + 2 * HZ) * (B + 2 * HY), X)
-
-    def turn_r(j, carry):
-        rr[j] = cflat[pl.ds(HZ * (B + 2 * HY) + HY + j, B, stride=B + 2 * HY), :]
-        return carry
-
-    lax.fori_loop(0, B, turn_r, 0)
+    src = cb if NSUB % 2 == 0 else ca
+    rflat = rr.reshape(B * B, X)
+
+    def last(z, carry):
+        at, up = slice(HY, HY + B), slice(4, 4 + B)
+        new = ((k0[z, up] * src[z, at]
+                + cym[z, up] * src[z, HY - 1 : HY - 1 + B])
+               - (cyp[z, up] * src[z, HY + 1 : HY + 1 + B]
+                  - czm[z, up] * src[z - 1, at])
+               - czp[z, up] * src[z + 1, at])
+        rflat[pl.ds(z - HZ, B, stride=B), :] = new
+        return carry
+
+    lax.fori_loop(HZ, HZ + B, last, 0)
+
     g0, gl = local_scan(rr, ay, by, ff, gg, iy)
     put_pair(gsy, 0, g0, gl)
     gry[g] = gsy[lax.rem(g, C)]
     for k in range(1, ny):
         to_y(gsy, gry, grsem.at[0], k).start()
 
-    wait_all(pry, ny - 1, psem.at[0, 1])
+    wait_all(pry.at[:, 0:PR], ny - 1, psem.at[0, 1])
     owner_matrix(ny, pry, my, yy, rf, rb)
 
     def base(j, carry):
@@ -427,7 +442,7 @@
             rsy.at[m], rety.at[yc], rtsem.at[0, 0], rtsem.at[0, 1],
             device_id=(p, b), device_id_type=MESH).start()
 
-    wait_all(prz, nz - 1, psem.at[1, 1])
+    wait_all(prz.at[:, 0:PR], nz - 1, psem.at[1, 1])
     owner_matrix(nz, prz, mz, yz, rf, rb)
 
     wait_all(rety, C - 1, rtsem.at[0, 1])
@@ -470,18 +485,23 @@
         out[j] = ff[j] + flo * lz[j] + fhi * hz[j]
         return carry
 
-    lax.fori_loop(0, B, end_z, 0)
-    store = pltpu.make_async_copy(out, o_hbm, lsem.at[4])
-    store.start()
-    for h in halo:
+    stores = []
+    for j in range(0, B, OUT):
+        lax.fori_loop(j, j + OUT, end_z, 0)
+        st = pltpu.make_async_copy(
+            out.at[j : j + OUT], o_hbm.at[j : j + OUT], lsem.at[4 + j // OUT])
+        st.start()
+        stores.append(st)
+    for h in edges + halo:
         h.wait_send()
-    wait_all(pry, ny - 1, psem.at[0, 0])
-    wait_all(prz, nz - 1, psem.at[1, 0])
+    wait_all(pry.at[:, 0:PR], ny - 1, psem.at[0, 0])
+    wait_all(prz.at[:, 0:PR], nz - 1, psem.at[1, 0])
     wait_all(gry, ny - 1, grsem.at[0, 0])
     wait_all(grz, nz - 1, grsem.at[1, 0])
     wait_all(rety, C - 1, rtsem.at[0, 0])
     wait_all(retz, C - 1, rtsem.at[1, 0])
-    store.wait()
+    for st in stores:
+        st.wait()
 
 
 def local(nz, ny, tracer, y_speed, z_speed, kappa):
@@ -496,15 +516,16 @@
     scratch = (
         [pad] * 4 + [blk] * 2 + [wgt] * 5
         + [blk] * 5 + [blk] * 5 + [blk] * 6
-        + [tiles(C, 24), tiles(C, 24), tiles(ny, 24), tiles(nz, 24)]
+        + [tiles(C, 16), tiles(C, 16), tiles(ny, 16), tiles(nz, 16)]
         + [tiles(C), tiles(C), tiles(ny), tiles(nz)]
         + [tiles(ny), tiles(ny + 1), tiles(ny + 1), tiles(ny + 1)]
         + [tiles(nz), tiles(nz + 1), tiles(nz + 1), tiles(nz + 1)]
         + [tiles(ny), tiles(ny)]
         + [tiles(C), tiles(C), tiles(C), tiles(C)]
-        + [pltpu.SemaphoreType.DMA((5,)), pltpu.SemaphoreType.DMA((24,)),
+        + [tiles(B), pltpu.VMEM((B, X), f32), pltpu.SemaphoreType.DMA((4 + B // OUT,)), pltpu.SemaphoreType.DMA((24,)),
            pltpu.SemaphoreType.DMA((24,)), pltpu.SemaphoreType.DMA((2, 2)),
-           pltpu.SemaphoreType.DMA((2, 2)), pltpu.SemaphoreType.DMA((2, 2))]
+           pltpu.SemaphoreType.DMA((2, 2)), pltpu.SemaphoreType.DMA((2, 2)),
+           pltpu.SemaphoreType.DMA((4,))]
     )
     return pl.pallas_call(
         functools.partial(kernel, nz, ny),
@@ -513,7 +534,7 @@
         out_specs=pl.BlockSpec(memory_space=pl.ANY),
         scratch_shapes=scratch,
         compiler_params=pltpu.CompilerParams(
-            collective_id=0, has_side_effects=True, vmem_limit_bytes=67043328),
+            collective_id=0, has_side_effects=True, vmem_limit_bytes=56000000),
     )(tracer, y_speed, z_speed, kappa)
 
 

time: 54.7 us -> 51.6 us (0.943)
  the two profiles are of different devices: /device:TPU:4 before, /device:TPU:24 now
where the time goes in v3:
time: 51.6 us; the launch traced here: 50.9 us
  Pallas kernels  50.1 us (97%)
  local copies, waits for them, and re-layouts  0.8 us (2%)
    pallas_call x1, Pallas kernels, local(): pl.pallas_call(functools.partial(kernel, nz, ny), out_shape=jax.ShapeDtyp...  50.1 us

profile of v3, /device:TPU:24, one launch (start us, length us, event | category | flops | bytes accessed | tf_op | source)
XLA Modules:
  0.0 50.9 jit_solution(6363406478432628925)
XLA Ops:
  0.0 50.1 %shard_map.46 = f32[32,32,128]{2,1,0:T(8,128)S(1)} custom-call(f32[32,32,128]{2,1,0:T(8,128)} %refs_0_.1, f32[32,32,128]{2,1,0:T(8,128)} %refs_1_.1, f32[32,32,128]{2,1,0:T(8,128)} %refs_2_.1, f32[32,32,128]{2,1,0:T(8,128)} %refs_3_.1), custom_call_target="tpu_custom_call" | custom-call | tf_op jit(solution)/shard_map/pallas_call | solution.py:530
  50.1 0.8 %copy.6 = f32[32,32,128]{2,1,0:T(8,128)} copy(f32[32,32,128]{2,1,0:T(8,128)S(1)} %shard_map.46) | data formatting | bytes 1048576

commit v4 on v3

--- a/solution.py
+++ b/solution.py
@@ -191,7 +191,7 @@
      psy, psz, pry, prz, gsy, gsz, gry, grz,
      my, yy, uy, vy, mz, yz, uo, vo, rf, rb,
      rsy, rsz, rety, retz,
-     kye, kze, lsem, hsend, hrecv, psem, grsem, rtsem, ksem) = refs
+     kye, kze, lsem, hsend, hrecv, psem, grsem, rtsem, ksem, ysem, zsem) = refs
     p = lax.axis_index("gz")
     g = lax.axis_index("gy")
 
@@ -202,17 +202,24 @@
         return lax.rem(g + k + ny, ny)
 
     bar = pltpu.get_barrier_semaphore()
-
-    def greet(pz, gy):
-        pl.semaphore_signal(bar, inc=1, device_id=(pz, gy), device_id_type=MESH)
-
-    for dz in (1, -1):
-        for dy in (1, -1):
-            greet(zi(dz), yi(dy))
-    for k in range(1, nz):
-        greet(zi(k), g)
-    for k in range(1, ny):
-        greet(p, yi(k))
+    neighbours = [(dz, dy) for dz in (1, 0, -1) for dy in (1, 0, -1) if dz or dy]
+    for dz, dy in neighbours:
+        pl.semaphore_signal(bar, inc=1, device_id=(zi(dz), yi(dy)), device_id_type=MESH)
+
+    def greet(r):
+        d = 1 << r
+        if 2 * d < ny:
+            for k in (d, -d):
+                pl.semaphore_signal(ysem.at[r], inc=1, device_id=(p, yi(k)), device_id_type=MESH)
+        if 2 * d < nz:
+            for k in (d, -d):
+                pl.semaphore_signal(zsem.at[r], inc=1, device_id=(zi(k), g), device_id_type=MESH)
+
+    def greeted(r):
+        if 2 << r < ny:
+            pl.semaphore_wait(ysem.at[r], 2)
+        if 2 << r < nz:
+            pl.semaphore_wait(zsem.at[r], 2)
 
     loads = [
         pltpu.make_async_copy(k_hbm, kz, lsem.at[0]),
@@ -223,7 +230,7 @@
     for ld in loads:
         ld.start()
 
-    pl.semaphore_wait(bar, 4 + (nz - 1) + (ny - 1))
+    pl.semaphore_wait(bar, len(neighbours))
 
     def near(d, size, pad, width):
         if d == 0:
@@ -253,6 +260,7 @@
     ]
     for h in edges + halo:
         h.start()
+    greet(0)
 
     loads[0].wait()
     kflat = kz.reshape(B * B, X)
@@ -267,6 +275,8 @@
     zfirst = jnp.where(p == 0, RATE, 0.0).astype(jnp.float32)
     zlast = jnp.where(p == nz - 1, RATE, 0.0).astype(jnp.float32)
 
+    greeted(0)
+    greet(1)
     factor(ky, yfirst, ylast, ay, by, iy, ly, hy, tmp)
     edges[0].wait_recv()
     below = kye.reshape(B * 8, X)[pl.ds(0, B, stride=8), :]
@@ -288,10 +298,15 @@
         part = ref.at[pl.ds(0, count)]
         pltpu.make_async_copy(part, part, sem).wait()
 
+    greeted(1)
+    greet(2)
+    factor(kz, zfirst, zlast, az, bz, iz, lz, hz, tmp)
+    greeted(2)
+    greet(3)
+    greeted(3)
     for k in range(1, ny):
         to_y(psy.at[:, 0:PR], pry.at[:, 0:PR], psem.at[0], k).start()
 
-    factor(kz, zfirst, zlast, az, bz, iz, lz, hz, tmp)
     edges[1].wait_recv()
     put_pair(psz, 0, lz[0] + 1.0 / (HALF_RATE * (kze[...] + kz[0])), hz[B - 1])
     put_pair(psz, 8, hz[0], hz[0])
@@ -525,7 +540,8 @@
         + [tiles(B), pltpu.VMEM((B, X), f32), pltpu.SemaphoreType.DMA((4 + B // OUT,)), pltpu.SemaphoreType.DMA((24,)),
            pltpu.SemaphoreType.DMA((24,)), pltpu.SemaphoreType.DMA((2, 2)),
            pltpu.SemaphoreType.DMA((2, 2)), pltpu.SemaphoreType.DMA((2, 2)),
-           pltpu.SemaphoreType.DMA((4,))]
+           pltpu.SemaphoreType.DMA((4,)),
+           pltpu.SemaphoreType.REGULAR((4,)), pltpu.SemaphoreType.REGULAR((4,))]
     )
     return pl.pallas_call(
         functools.partial(kernel, nz, ny),

time: 51.6 us -> 50.9 us (0.986); the launches traced: 50.9 us -> 50.8 us
  no operation moved by 1% of the time
where the time goes in v4:
time: 50.9 us; the launch traced here: 50.8 us
  Pallas kernels  50 us (98%)
  local copies, waits for them, and re-layouts  0.8 us (2%)
    pallas_call x1, Pallas kernels, local(): pl.pallas_call(functools.partial(kernel, nz, ny), out_shape=jax.ShapeDtyp...  50 us

profile of v4, /device:TPU:24, one launch (start us, length us, event | category | flops | bytes accessed | tf_op | source)
XLA Modules:
  0.0 50.8 jit_solution(3366339303649403281)
XLA Ops:
  0.0 50.0 %shard_map.46 = f32[32,32,128]{2,1,0:T(8,128)S(1)} custom-call(f32[32,32,128]{2,1,0:T(8,128)} %refs_0_.1, f32[32,32,128]{2,1,0:T(8,128)} %refs_1_.1, f32[32,32,128]{2,1,0:T(8,128)} %refs_2_.1, f32[32,32,128]{2,1,0:T(8,128)} %refs_3_.1), custom_call_target="tpu_custom_call" | custom-call | tf_op jit(solution)/shard_map/pallas_call | solution.py:546
  50.0 0.8 %copy.6 = f32[32,32,128]{2,1,0:T(8,128)} copy(f32[32,32,128]{2,1,0:T(8,128)S(1)} %shard_map.46) | data formatting | bytes 1048576

commit v5 on v4

--- a/solution.py
+++ b/solution.py
@@ -278,6 +278,8 @@
     greeted(0)
     greet(1)
     factor(ky, yfirst, ylast, ay, by, iy, ly, hy, tmp)
+    greeted(1)
+    greet(2)
     edges[0].wait_recv()
     below = kye.reshape(B * 8, X)[pl.ds(0, B, stride=8), :]
     put_pair(psy, 0, ly[0] + 1.0 / (HALF_RATE * (below + ky[0])), hy[B - 1])
@@ -298,26 +300,17 @@
         part = ref.at[pl.ds(0, count)]
         pltpu.make_async_copy(part, part, sem).wait()
 
-    greeted(1)
-    greet(2)
-    factor(kz, zfirst, zlast, az, bz, iz, lz, hz, tmp)
     greeted(2)
     greet(3)
     greeted(3)
     for k in range(1, ny):
         to_y(psy.at[:, 0:PR], pry.at[:, 0:PR], psem.at[0], k).start()
 
-    edges[1].wait_recv()
-    put_pair(psz, 0, lz[0] + 1.0 / (HALF_RATE * (kze[...] + kz[0])), hz[B - 1])
-    put_pair(psz, 8, hz[0], hz[0])
-    prz[p] = psz[lax.rem(p, C)]
 
     for ld in loads[1:]:
         ld.wait()
     for h in halo:
         h.wait_recv()
-    for k in range(1, nz):
-        to_z(psz.at[:, 0:PR], prz.at[:, 0:PR], psem.at[1], k).start()
 
     zero3 = jnp.zeros((HZ, B + 2 * HY, X), jnp.float32)
     zero_row = jnp.zeros((HY, X), jnp.float32)
@@ -435,15 +428,16 @@
     for k in range(1, ny):
         to_y(gsy, gry, grsem.at[0], k).start()
 
+    factor(kz, zfirst, zlast, az, bz, iz, lz, hz, tmp)
+    edges[1].wait_recv()
+    put_pair(psz, 0, lz[0] + 1.0 / (HALF_RATE * (kze[...] + kz[0])), hz[B - 1])
+    put_pair(psz, 8, hz[0], hz[0])
+    prz[p] = psz[lax.rem(p, C)]
+    for k in range(1, nz):
+        to_z(psz.at[:, 0:PR], prz.at[:, 0:PR], psem.at[1], k).start()
+
     wait_all(pry.at[:, 0:PR], ny - 1, psem.at[0, 1])
     owner_matrix(ny, pry, my, yy, rf, rb)
-
-    def base(j, carry):
-        ff[j] = (ff[j] + gg[j]) * inv_now[j]
-        return carry
-
-    inv_now = iy
-    lax.fori_loop(0, B, base, 0)
 
     wait_all(gry, ny - 1, grsem.at[0, 1])
     owner_scan(ny, gry, my, uy, vy)
@@ -457,8 +451,11 @@
             rsy.at[m], rety.at[yc], rtsem.at[0, 0], rtsem.at[0, 1],
             device_id=(p, b), device_id_type=MESH).start()
 
-    wait_all(prz.at[:, 0:PR], nz - 1, psem.at[1, 1])
-    owner_matrix(nz, prz, mz, yz, rf, rb)
+    def base(j, carry):
+        ff[j] = (ff[j] + gg[j]) * iy[j]
+        return carry
+
+    lax.fori_loop(0, B, base, 0)
 
     wait_all(rety, C - 1, rtsem.at[0, 1])
     flo, fhi = get_pair(rety)
@@ -475,13 +472,15 @@
     grz[p] = gsz[lax.rem(p, C)]
     for k in range(1, nz):
         to_z(gsz, grz, grsem.at[1], k).start()
-    inv_now = iz
 
     def base_z(j, carry):
         ff[j] = (ff[j] + gg[j]) * iz[j]
         return carry
 
     lax.fori_loop(0, B, base_z, 0)
+    wait_all(prz.at[:, 0:PR], nz - 1, psem.at[1, 1])
+    owner_matrix(nz, prz, mz, yz, rf, rb)
+
     wait_all(grz, nz - 1, grsem.at[1, 1])
     owner_scan(nz, grz, mz, uo, vo)
     zc = lax.rem(p, C)

time: 50.9 us -> 50.8 us (level)
  no operation moved by 1% of the time
where the time goes in v5:
time: 50.8 us; the launch traced here: 50.7 us
  Pallas kernels  49.9 us (98%)
  local copies, waits for them, and re-layouts  0.8 us (2%)
    pallas_call x1, Pallas kernels, local(): pl.pallas_call(functools.partial(kernel, nz, ny), out_shape=jax.ShapeDtyp...  49.9 us

profile of v5, /device:TPU:24, one launch (start us, length us, event | category | flops | bytes accessed | tf_op | source)
XLA Modules:
  0.0 50.7 jit_solution(14576995193500737056)
XLA Ops:
  0.0 49.9 %shard_map.46 = f32[32,32,128]{2,1,0:T(8,128)S(1)} custom-call(f32[32,32,128]{2,1,0:T(8,128)} %refs_0_.1, f32[32,32,128]{2,1,0:T(8,128)} %refs_1_.1, f32[32,32,128]{2,1,0:T(8,128)} %refs_2_.1, f32[32,32,128]{2,1,0:T(8,128)} %refs_3_.1), custom_call_target="tpu_custom_call" | custom-call | tf_op jit(solution)/shard_map/pallas_call | solution.py:545
  49.9 0.8 %copy.6 = f32[32,32,128]{2,1,0:T(8,128)} copy(f32[32,32,128]{2,1,0:T(8,128)S(1)} %shard_map.46) | data formatting | bytes 1048576

commit v6 on v5

--- a/solution.py
+++ b/solution.py
@@ -240,7 +240,7 @@
         return slice(0, width), slice(pad + size, pad + size + width)
 
     halo = []
-    for dz, dy in ((0, 1), (0, -1), (1, 0), (-1, 0), (1, 1), (1, -1), (-1, 1), (-1, -1)):
+    for dz, dy in ((1, 1), (1, -1), (-1, 1), (-1, -1), (0, 1), (0, -1), (1, 0), (-1, 0)):
         for src, dst, wz, wy in ((c_hbm, ca, 4, 4), (v_hbm, vv, 3, 4), (w_hbm, ww, 4, 3)):
             if dz and dy:
                 wz, wy = 3, 3

time: 50.8 us -> 50.8 us (level)
  no operation moved by 1% of the time
where the time goes in v6:
time: 50.8 us; the launch traced here: 50.7 us
  Pallas kernels  49.9 us (98%)
  local copies, waits for them, and re-layouts  0.8 us (2%)
    pallas_call x1, Pallas kernels, local(): pl.pallas_call(functools.partial(kernel, nz, ny), out_shape=jax.ShapeDtyp...  49.9 us

profile of v6, /device:TPU:24, one launch (start us, length us, event | category | flops | bytes accessed | tf_op | source)
XLA Modules:
  0.0 50.7 jit_solution(5198654410075523501)
XLA Ops:
  0.0 49.9 %shard_map.46 = f32[32,32,128]{2,1,0:T(8,128)S(1)} custom-call(f32[32,32,128]{2,1,0:T(8,128)} %refs_0_.1, f32[32,32,128]{2,1,0:T(8,128)} %refs_1_.1, f32[32,32,128]{2,1,0:T(8,128)} %refs_2_.1, f32[32,32,128]{2,1,0:T(8,128)} %refs_3_.1), custom_call_target="tpu_custom_call" | custom-call | tf_op jit(solution)/shard_map/pallas_call | solution.py:545
  49.9 0.8 %copy.6 = f32[32,32,128]{2,1,0:T(8,128)} copy(f32[32,32,128]{2,1,0:T(8,128)S(1)} %shard_map.46) | data formatting | bytes 1048576

commit v7 on v5

--- a/solution.py
+++ b/solution.py
@@ -303,14 +303,14 @@
     greeted(2)
     greet(3)
     greeted(3)
-    for k in range(1, ny):
-        to_y(psy.at[:, 0:PR], pry.at[:, 0:PR], psem.at[0], k).start()
 
 
     for ld in loads[1:]:
         ld.wait()
     for h in halo:
         h.wait_recv()
+    for k in range(1, ny):
+        to_y(psy.at[:, 0:PR], pry.at[:, 0:PR], psem.at[0], k).start()
 
     zero3 = jnp.zeros((HZ, B + 2 * HY, X), jnp.float32)
     zero_row = jnp.zeros((HY, X), jnp.float32)

time: 50.8 us -> 50.9 us (level)
  no operation moved by 1% of the time
where the time goes in v7:
time: 50.9 us; the launch traced here: 50.8 us
  Pallas kernels  50 us (98%)
  local copies, waits for them, and re-layouts  0.8 us (2%)
    pallas_call x1, Pallas kernels, local(): pl.pallas_call(functools.partial(kernel, nz, ny), out_shape=jax.ShapeDtyp...  50 us

profile of v7, /device:TPU:24, one launch (start us, length us, event | category | flops | bytes accessed | tf_op | source)
XLA Modules:
  0.0 50.8 jit_solution(13020861544998190321)
XLA Ops:
  0.0 50.0 %shard_map.46 = f32[32,32,128]{2,1,0:T(8,128)S(1)} custom-call(f32[32,32,128]{2,1,0:T(8,128)} %refs_0_.1, f32[32,32,128]{2,1,0:T(8,128)} %refs_1_.1, f32[32,32,128]{2,1,0:T(8,128)} %refs_2_.1, f32[32,32,128]{2,1,0:T(8,128)} %refs_3_.1), custom_call_target="tpu_custom_call" | custom-call | tf_op jit(solution)/shard_map/pallas_call | solution.py:545
  50.0 0.8 %copy.6 = f32[32,32,128]{2,1,0:T(8,128)} copy(f32[32,32,128]{2,1,0:T(8,128)S(1)} %shard_map.46) | data formatting | bytes 1048576
